TPU v7x, 32 devices: a whole 2x2x4 slice. The times are simulated.
32 devices in a mesh: ctx: 4 (over y, core), head: 4 (over z), wide: 2 (over x).
Axes of the slice: x: 2, y: 2, z: 4, core: 2. Of those that a mesh axis runs over, the one named last changes fastest.
Arguments:
- query_rows: bfloat16 [2, 1024, 1024], P('wide', 'ctx', 'head'), may hold values from -105 to 105
- key_rows: bfloat16 [2, 1024, 1024], P('wide', 'ctx', 'head'), may hold values from -4.5 to 4.5
- value_rows: bfloat16 [2, 1024, 1024], P('wide', 'ctx', 'head'), may hold values from -6 to 6
- grad_out: bfloat16 [2, 1024, 1024], P('wide', 'ctx', 'head'), may hold values from -6 to 6
- segment: int32 [2, 1024], P('wide', 'ctx'), may hold values from 0 to 7, never falling along the last dimension, each value on 1 to 256 neighbouring positions
- frames: bfloat16 [2, 1024, 4096], P(None, 'ctx', 'wide'), may hold values from -6 to 6
Outputs:
- grad_query: bfloat16 [2, 1024, 1024], P('wide', 'ctx', 'head')
- grad_key: bfloat16 [2, 1024, 1024], P('wide', 'ctx', 'head')
- grad_value: bfloat16 [2, 1024, 1024], P('wide', 'ctx', 'head')
- grad_wq: float32 [2, 2048, 1024], P('wide', 'ctx', 'head')
Inputs may be any that keep to these rules, and one draw needn't show every extreme that they name: Ids never fall along a recording; each segment spans 1 to 256 frames and one spans exactly 256.
All inputs are finite; a program needn't handle non-finite values.
Results may differ from a plain program's by a relative error of at most 0.01.
Values may be sent and summed in bfloat16 or wider, within the bound.
No kernel may reach another device: no remote copies, remote signals or barrier semaphores. Data moves between devices by JAX's collectives and lax.ppermute only.
A program may use at most 64 MiB of HBM per device.

v0:
```python
import jax
import jax.numpy as jnp
from jax import lax
from jax.sharding import PartitionSpec as P

HD = 128


def shifted(value, axis, steps):
    count = lax.axis_size(axis)
    initial, last = (max(0, -steps), min(count, count - steps))
    return lax.ppermute(value, axis, [(source, source + steps) for source in range(initial, last)])


def head_scores(left_heads, right_heads):
    return jnp.einsum("ihd,jhd->hij", left_heads, right_heads, preferred_element_type=jnp.float32)


def shards(query_rows, key_rows, value_rows, grad_out, segment, frames):
    length = query_rows.shape[1]
    columns = query_rows.shape[2]
    head_count = columns // HD
    factor = HD ** (-0.5)
    ctx_index = lax.axis_index("ctx")
    ctx_count = lax.axis_size("ctx")
    query_heads = query_rows.reshape(length, head_count, HD)
    key_heads = key_rows.reshape(length, head_count, HD)
    value_heads = value_rows.reshape(length, head_count, HD)
    grad_heads = grad_out.reshape(length, head_count, HD)
    own_segment = segment[0]
    prior_keys, prior_values, prior_segment = shifted((key_rows, value_rows, segment), "ctx", 1)
    prior_key_heads = prior_keys.reshape(length, head_count, HD)
    prior_value_heads = prior_values.reshape(length, head_count, HD)
    places = jnp.arange(length, dtype=jnp.int32)
    own_mask = (own_segment[:, None] == own_segment[None, :]) & (places[None, :] <= places[:, None])
    prior_mask = (own_segment[:, None] == prior_segment[0][None, :]) & (ctx_index > 0)
    own_scores = head_scores(query_heads, key_heads) * factor
    prior_scores = head_scores(query_heads, prior_key_heads) * factor
    row_max = jnp.maximum(
        jnp.max(jnp.where(own_mask, own_scores, -jnp.inf), axis=2, keepdims=True),
        jnp.max(jnp.where(prior_mask, prior_scores, -jnp.inf), axis=2, keepdims=True),
    )
    row_total = jnp.sum(
        jnp.where(own_mask, jnp.exp(own_scores - row_max), 0.0), axis=2, keepdims=True
    ) + jnp.sum(jnp.where(prior_mask, jnp.exp(prior_scores - row_max), 0.0), axis=2, keepdims=True)
    log_total = row_max + jnp.log(row_total)
    own_prob = jnp.where(own_mask, jnp.exp(own_scores - log_total), 0.0)
    prior_prob = jnp.where(prior_mask, jnp.exp(prior_scores - log_total), 0.0)
    own_grad_prob = head_scores(grad_heads, value_heads)
    prior_grad_prob = head_scores(grad_heads, prior_value_heads)
    row_delta = jnp.sum(own_prob * own_grad_prob, axis=2, keepdims=True) + jnp.sum(
        prior_prob * prior_grad_prob, axis=2, keepdims=True
    )
    own_grad_score = (own_prob * (own_grad_prob - row_delta)).astype(jnp.bfloat16)
    prior_grad_score = (prior_prob * (prior_grad_prob - row_delta)).astype(jnp.bfloat16)
    own_prob_low = own_prob.astype(jnp.bfloat16)
    grad_query_heads = (
        jnp.einsum("hij,jhd->ihd", own_grad_score, key_heads, preferred_element_type=jnp.float32)
        + jnp.einsum(
            "hij,jhd->ihd", prior_grad_score, prior_key_heads, preferred_element_type=jnp.float32
        )
    ) * factor
    grad_query = grad_query_heads.astype(jnp.bfloat16).reshape(1, length, columns)
    own_key_grad = jnp.einsum(
        "hij,ihd->jhd", own_grad_score, query_heads, preferred_element_type=jnp.float32
    )
    own_value_grad = jnp.einsum(
        "hij,ihd->jhd", own_prob_low, grad_heads, preferred_element_type=jnp.float32
    )
    prior_key_grad = jnp.einsum(
        "hij,ihd->jhd", prior_grad_score, query_heads, preferred_element_type=jnp.float32
    )
    prior_value_grad = jnp.einsum(
        "hij,ihd->jhd",
        prior_prob.astype(jnp.bfloat16),
        grad_heads,
        preferred_element_type=jnp.float32,
    )
    later_key_grad, later_value_grad = shifted((prior_key_grad, prior_value_grad), "ctx", -1)
    grad_key = (
        ((own_key_grad + later_key_grad) * factor).astype(jnp.bfloat16).reshape(1, length, columns)
    )
    grad_value = (
        (own_value_grad + later_value_grad).astype(jnp.bfloat16).reshape(1, length, columns)
    )
    width = frames.shape[2]
    row_block = width // ctx_count
    panel_sum = jnp.einsum(
        "rtd,rtc->dc",
        frames,
        lax.all_gather(grad_query, "wide", axis=0, tiled=True),
        preferred_element_type=jnp.float32,
    )
    grad_wq = lax.psum_scatter(panel_sum, "ctx", scatter_dimension=0, tiled=True).reshape(
        1, row_block, columns
    )
    return (grad_query, grad_key, grad_value, grad_wq)


def solution(mesh):
    return jax.shard_map(
        shards,
        mesh=mesh,
        in_specs=(
            P("wide", "ctx", "head"),
            P("wide", "ctx", "head"),
            P("wide", "ctx", "head"),
            P("wide", "ctx", "head"),
            P("wide", "ctx"),
            P(None, "ctx", "wide"),
        ),
        out_specs=(
            P("wide", "ctx", "head"),
            P("wide", "ctx", "head"),
            P("wide", "ctx", "head"),
            P("wide", "ctx", "head"),
        ),
        check_vma=False,
    )
```

profile of v0, /device:TPU:0, one launch (start us, length us, event | category | flops | bytes accessed | tf_op | source)
XLA Modules:
  0.0 79.4 jit_solution(1340995519553160902)
XLA Ops:
  7.2 2.5 %collective-permute-start = (s32[1,256]{1,0:T(1,128)}, s32[1,256]{1,0:T(1,128)S(1)}, u32[]{:S(2)}, u32[]{:S(2)}) collective-permute-start(s32[1,256]{1,0:T(1,128)} %param.10), channel_id=1, source_target_pairs={{0,8},{8,16},{16,24},{1,9},{9,17},{17,25},{2,10},{10,18},{18,26},{... | collective-permute-start | bytes 3080 | tf_op jit(solution)/shard_map/ppermute | solution.py:12
  9.8 1.7 %copy.64 = bf16[1,256,256]{1,2,0:T(8,128)(2,1)} copy(bf16[1,256,256]{2,1,0:T(8,128)(2,1)} %param.8) | data formatting | bytes 262144 | tf_op args[2]
  11.4 5.2 %collective-permute-start.2 = (bf16[1,256,256]{1,2,0:T(8,128)(2,1)}, bf16[1,256,256]{1,2,0:T(8,128)(2,1)}, u32[]{:S(2)}, u32[]{:S(2)}) collective-permute-start(bf16[1,256,256]{1,2,0:T(8,128)(2,1)} %copy.64), channel_id=1, source_target_pairs={{0,8},{8,16},{16,24},{1,9},{9,17},{17,25},{2,10},{10,18},{18,26},{... | collective-permute-start | bytes 393224 | tf_op jit(solution)/shard_map/ppermute | solution.py:12
  16.6 1.0 %copy.93 = bf16[1,256,256]{1,2,0:T(8,128)(2,1)S(1)} copy(bf16[1,256,256]{2,1,0:T(8,128)(2,1)} %param.7) | data formatting | bytes 262144 | tf_op jit(solution)/shard_map/reshape | solution.py:27
  17.6 1.3 %collective-permute-start.1 = (bf16[1,256,256]{1,2,0:T(8,128)(2,1)S(1)}, bf16[1,256,256]{1,2,0:T(8,128)(2,1)S(1)}, u32[]{:S(2)}, u32[]{:S(2)}) collective-permute-start(bf16[1,256,256]{1,2,0:T(8,128)(2,1)S(1)} %copy.93), channel_id=1, source_target_pairs={{0,8},{8,16},{16,24},{1,9},{9,17},{17,25},{2,10},{10,18},{18,26},{... | collective-permute-start | bytes 393224 | tf_op jit(solution)/shard_map/ppermute | solution.py:12
  18.9 0.9 %reshape.69 = bf16[256,2,128]{2,1,0:T(2,128)(2,1)S(1)} reshape(bf16[1,256,256]{2,1,0:T(8,128)(2,1)} %param.8) | data formatting | bytes 262144 | tf_op jit(solution)/shard_map/reshape | solution.py:28
  19.9 0.9 %reshape.68 = bf16[256,2,128]{2,1,0:T(2,128)(2,1)S(1)} reshape(bf16[1,256,256]{2,1,0:T(8,128)(2,1)} %param.9) | data formatting | bytes 262144 | tf_op jit(solution)/shard_map/reshape | solution.py:29
  20.8 1.0 %fusion.18 = f32[2,256,256]{1,2,0:T(8,128)} fusion(bf16[256,2,128]{2,1,0:T(2,128)(2,1)S(1)} %reshape.69, bf16[256,2,128]{2,1,0:T(2,128)(2,1)S(1)} %reshape.68), kind=kOutput, calls=%fused_computation.36 | convolution fusion | flops 33554432 | bytes 786432 | tf_op jit(solution)/shard_map/ihd,jhd->hij/dot_general | solution.py:16
  21.8 0.9 %reshape.65 = bf16[256,2,128]{2,1,0:T(2,128)(2,1)S(1)} reshape(bf16[1,256,256]{2,1,0:T(8,128)(2,1)} %param.6) | data formatting | bytes 262144 | tf_op jit(solution)/shard_map/reshape | solution.py:26
  23.9 1.2 %select_reduce_fusion.2 = (f32[2,256]{1,0:T(2,128)S(1)}, f32[2,256,256]{1,2,0:T(8,128)S(1)}) fusion(pred[256,256]{0,1:T(8,128)(4,1)S(1)} %get-tuple-element.22, bf16[256,2,128]{0,2,1:T(8,128)(2,1)} %bitcast.50, bf16[256,2,128]{2,1,0:T(2,128)(2,1)S(1)} %reshape.65), kind=kOutput, calls=%fused_computation.23 | convolution fusion | flops 33947136 | bytes 854016 | tf_op jit(solution)/shard_map/ihd,jhd->hij/dot_general | solution.py:16
  25.4 1.4 %multiply_reduce_fusion = (f32[2,256]{1,0:T(2,128)S(1)}, f32[2,256]{1,0:T(2,128)S(1)}, f32[2,256,256]{1,2,0:T(8,128)S(1)}) fusion(f32[2,256,256]{1,2,0:T(8,128)S(1)} %get-tuple-element.27, f32[2,256]{1,0:T(2,128)S(1)} %log_add_fusion, pred[256,256]{0,1:T(8,128)(4,1)S(1)} %get-tuple-element.22, f32[2,256,256]{1,2,0:T(8,128)S(1)} %copy-done.1, ...), kind=kOutput, calls=%fused_computation.17 | convolution fusion | flops 34601984 | bytes 2496512 | tf_op jit(solution)/shard_map/ihd,jhd->hij/dot_general | solution.py:16
  28.0 0.8 %fusion.6 = bf16[2,256,128]{1,2,0:T(8,128)(2,1)} fusion(f32[2,256,128]{1,2,0:T(8,128)S(1)} %fusion.31, bf16[256,2,128]{0,2,1:T(8,128)(2,1)S(1)} %bitcast.51, bf16[2,256,256]{1,2,0:T(8,128)(2,1)S(1)} %get-tuple-element.20), kind=kOutput, calls=%fused_computation.14 | convolution fusion | flops 33751040 | bytes 786432 | tf_op jit(solution)/shard_map/hij,jhd->ihd/dot_general | solution.py:59
  28.9 1.7 %copy.80 = bf16[1,256,256]{2,1,0:T(8,128)(2,1)} copy(bf16[1,256,256]{1,2,0:T(8,128)(2,1)} %bitcast.49) | data formatting | bytes 262144
  30.5 6.3 %all_gather.3 = bf16[2,256,256]{2,1,0:T(8,128)(2,1)S(1)} all-gather(bf16[1,256,256]{2,1,0:T(8,128)(2,1)} %copy.80), channel_id=1, replica_groups=mesh['ctx'=4,'head'=4,'wide'=2] {'wide'}, dimensions={0}, use_global_device_ids=true | all-gather | bytes 393216 | tf_op jit(solution)/shard_map/all_gather | solution.py:91
  36.8 2.1 %convolution_bitcast_fusion = f32[2048,256]{0,1:T(8,128)} fusion(bf16[2,256,256]{2,1,0:T(8,128)(2,1)S(1)} %all_gather.3, bf16[2,256,2048]{2,1,0:T(8,128)(2,1)S(1)} %copy-done), kind=kOutput, calls=%fused_computation | convolution fusion | flops 536870912 | bytes 4456448 | tf_op jit(solution)/shard_map/rtd,rtc->dc/dot_general | solution.py:88
  39.2 1.4 %collective-permute-start.4 = (f32[256,2,128]{0,2,1:T(8,128)S(1)}, f32[256,2,128]{0,2,1:T(8,128)S(1)}, u32[]{:S(2)}, u32[]{:S(2)}) collective-permute-start(f32[256,2,128]{0,2,1:T(8,128)S(1)} %convolution_bitcast_fusion.1), channel_id=1, source_target_pairs={{8,0},{16,8},{24,16},{9,1},{17,9},{25,17},{10,2},{18,10},{26,18},{... | collective-permute-start | bytes 786440 | tf_op jit(solution)/shard_map/ppermute | solution.py:12
  40.6 1.9 %convolution_bitcast_fusion.3 = f32[256,2,128]{0,2,1:T(8,128)} fusion(bf16[2,256,256]{1,2,0:T(8,128)(2,1)} %copy-done.4, bf16[256,2,128]{2,1,0:T(2,128)(2,1)S(1)} %reshape.65), kind=kOutput, calls=%fused_computation.8 | convolution fusion | flops 33554432 | bytes 655360 | tf_op jit(solution)/shard_map/hij,ihd->jhd/dot_general | solution.py:70
  42.5 1.3 %collective-permute-start.3 = (f32[256,2,128]{0,2,1:T(8,128)}, f32[256,2,128]{0,2,1:T(8,128)}, u32[]{:S(2)}, u32[]{:S(2)}) collective-permute-start(f32[256,2,128]{0,2,1:T(8,128)} %convolution_bitcast_fusion.3), channel_id=1, source_target_pairs={{8,0},{16,8},{24,16},{9,1},{17,9},{25,17},{10,2},{18,10},{26,18},{... | collective-permute-start | bytes 786440 | tf_op jit(solution)/shard_map/ppermute | solution.py:12
  44.0 0.8 copy.82
  44.8 2.3 %collective-permute-done.3 = f32[256,2,128]{0,2,1:T(8,128)} collective-permute-done((f32[256,2,128]{0,2,1:T(8,128)}, f32[256,2,128]{0,2,1:T(8,128)}, u32[]{:S(2)}, u32[]{:S(2)}) %collective-permute-start.3) | collective-permute-done | bytes 262176 | tf_op jit(solution)/shard_map/ppermute | solution.py:12
  47.1 1.2 %fusion.4 = bf16[256,2,128]{0,2,1:T(8,128)(2,1)S(1)} fusion(f32[256,2,128]{0,2,1:T(8,128)} %collective-permute-done.3, bf16[2,256,256]{1,2,0:T(8,128)(2,1)S(1)} %copy-done.3, bf16[256,2,128]{2,1,0:T(2,128)(2,1)S(1)} %reshape.65), kind=kOutput, calls=%fused_computation.12 | convolution fusion | flops 33751040 | bytes 786432 | tf_op jit(solution)/shard_map/hij,ihd->jhd/dot_general | solution.py:64
  48.3 0.8 copy.81
  49.1 21.4 %reduce-scatter.2.cloned.1.call-done = f32[512,256]{0,1:T(8,128)} async-done(((f32[2048,256]{0,1:T(8,128)}), f32[512,256]{0,1:T(8,128)}) %reduce-scatter.2.cloned.1.call-update) | async-done | bytes 524304 | tf_op jit(solution)/shard_map/reduce_scatter | solution.py:94
  70.5 2.0 %copy.83 = f32[1,512,256]{2,1,0:T(8,128)} copy(f32[1,512,256]{1,2,0:T(8,128)} %bitcast.47) | data formatting | bytes 1048576
  (36 shorter events, 3.1 us)
Async XLA Ops:
  7.2 29.6 %copy-start = (bf16[2,256,2048]{2,1,0:T(8,128)(2,1)S(1)}, bf16[2,256,2048]{2,1,0:T(8,128)(2,1)}, u32[]{:S(2)}) copy-start(bf16[2,256,2048]{2,1,0:T(8,128)(2,1)} %param.11) | copy-start | bytes 6291460
  7.2 15.6 %copy-start.9 = (s32[1,256]{1,0:T(1,128)S(1)}, s32[1,256]{1,0:T(1,128)}, u32[]{:S(2)}) copy-start(s32[1,256]{1,0:T(1,128)} %param.10) | copy-start | bytes 3076
  7.2 63.3 %reduce-scatter.2.cloned.1.call-start = ((), (), s32[]{:S(2)}) async-start(), calls=%async_computation.1 | async-start | bytes 2621440 | tf_op jit(solution)/shard_map/reduce_scatter | solution.py:94
  7.2 15.6 %collective-permute-start = (s32[1,256]{1,0:T(1,128)}, s32[1,256]{1,0:T(1,128)S(1)}, u32[]{:S(2)}, u32[]{:S(2)}) collective-permute-start(s32[1,256]{1,0:T(1,128)} %param.10), channel_id=1, source_target_pairs={{0,8},{8,16},{16,24},{1,9},{9,17},{17,25},{2,10},{10,18},{18,26},{... | collective-permute-start | bytes 3080 | tf_op jit(solution)/shard_map/ppermute | solution.py:12
  11.4 13.9 %collective-permute-start.2 = (bf16[1,256,256]{1,2,0:T(8,128)(2,1)}, bf16[1,256,256]{1,2,0:T(8,128)(2,1)}, u32[]{:S(2)}, u32[]{:S(2)}) collective-permute-start(bf16[1,256,256]{1,2,0:T(8,128)(2,1)} %copy.64), channel_id=1, source_target_pairs={{0,8},{8,16},{16,24},{1,9},{9,17},{17,25},{2,10},{10,18},{18,26},{... | collective-permute-start | bytes 393224 | tf_op jit(solution)/shard_map/ppermute | solution.py:12
  17.6 5.7 %copy-start.5 = (bf16[1,256,256]{1,2,0:T(8,128)(2,1)}, bf16[1,256,256]{1,2,0:T(8,128)(2,1)S(1)}, u32[]{:S(2)}) copy-start(bf16[1,256,256]{1,2,0:T(8,128)(2,1)S(1)} %copy.93) | copy-start | bytes 393220
  17.6 5.6 %collective-permute-start.1 = (bf16[1,256,256]{1,2,0:T(8,128)(2,1)S(1)}, bf16[1,256,256]{1,2,0:T(8,128)(2,1)S(1)}, u32[]{:S(2)}, u32[]{:S(2)}) collective-permute-start(bf16[1,256,256]{1,2,0:T(8,128)(2,1)S(1)} %copy.93), channel_id=1, source_target_pairs={{0,8},{8,16},{16,24},{1,9},{9,17},{17,25},{2,10},{10,18},{18,26},{... | collective-permute-start | bytes 393224 | tf_op jit(solution)/shard_map/ppermute | solution.py:12
  22.8 2.6 %copy-start.1 = (f32[2,256,256]{1,2,0:T(8,128)S(1)}, f32[2,256,256]{1,2,0:T(8,128)}, u32[]{:S(2)}) copy-start(f32[2,256,256]{1,2,0:T(8,128)} %fusion.18) | copy-start | bytes 1572868
  23.3 0.7 copy-start.7
  25.4 2.4 %copy-start.6 = (bf16[1,256,256]{1,2,0:T(8,128)(2,1)S(1)}, bf16[1,256,256]{1,2,0:T(8,128)(2,1)}, u32[]{:S(2)}) copy-start(bf16[1,256,256]{1,2,0:T(8,128)(2,1)} %copy-done.5) | copy-start | bytes 393220
  26.8 1.2 %copy-start.8 = (bf16[1,256,256]{1,2,0:T(8,128)(2,1)S(1)}, bf16[1,256,256]{1,2,0:T(8,128)(2,1)}, u32[]{:S(2)}) copy-start(bf16[1,256,256]{1,2,0:T(8,128)(2,1)} %copy-done.7) | copy-start | bytes 393220
  27.1 0.7 copy-start.2
  27.1 0.9 %copy-start.4 = (bf16[2,256,256]{1,2,0:T(8,128)(2,1)}, bf16[2,256,256]{1,2,0:T(8,128)(2,1)S(1)}, u32[]{:S(2)}) copy-start(bf16[2,256,256]{1,2,0:T(8,128)(2,1)S(1)} %get-tuple-element.20) | copy-start | bytes 786436
  39.1 8.0 %copy-start.3 = (bf16[2,256,256]{1,2,0:T(8,128)(2,1)S(1)}, bf16[2,256,256]{1,2,0:T(8,128)(2,1)}, u32[]{:S(2)}) copy-start(bf16[2,256,256]{1,2,0:T(8,128)(2,1)} %copy-done.2) | copy-start | bytes 786436
  39.2 4.6 %collective-permute-start.4 = (f32[256,2,128]{0,2,1:T(8,128)S(1)}, f32[256,2,128]{0,2,1:T(8,128)S(1)}, u32[]{:S(2)}, u32[]{:S(2)}) collective-permute-start(f32[256,2,128]{0,2,1:T(8,128)S(1)} %convolution_bitcast_fusion.1), channel_id=1, source_target_pairs={{8,0},{16,8},{24,16},{9,1},{17,9},{25,17},{10,2},{18,10},{26,18},{... | collective-permute-start | bytes 786440 | tf_op jit(solution)/shard_map/ppermute | solution.py:12
  42.5 4.6 %collective-permute-start.3 = (f32[256,2,128]{0,2,1:T(8,128)}, f32[256,2,128]{0,2,1:T(8,128)}, u32[]{:S(2)}, u32[]{:S(2)}) collective-permute-start(f32[256,2,128]{0,2,1:T(8,128)} %convolution_bitcast_fusion.3), channel_id=1, source_target_pairs={{8,0},{16,8},{24,16},{9,1},{17,9},{25,17},{10,2},{18,10},{26,18},{... | collective-permute-start | bytes 786440 | tf_op jit(solution)/shard_map/ppermute | solution.py:12
Sparse Core Ops, SparseCore 0:
  39.0 31.4 reduce-scatter.1
where the time goes:
time: 79.9 us; the launch traced here: 79.4 us
  waiting for transfers between devices  23.8 us (30%)
  between operations  14.3 us (18%)
  local copies, waits for them, and re-layouts  12.1 us (15%)
  starting transfers between devices  11.7 us (15%)
  matrix products  10.5 us (13%)
  blocking collectives  6.28 us (8%)
    reduce_scatter x1, waiting for transfers between devices, shards(): lax.psum_scatter(panel_sum, 'ctx', scatter_dimension=0, tiled=True)  21.4 us
    ppermute x5, starting transfers between devices, shifted(): lax.ppermute(value, axis, [(source, source + steps) for source in range(i...  11.7 us
    unnamed x25, local copies, waits for them, and re-layouts  8.25 us
    all_gather x1, blocking collectives, shards(): lax.all_gather(grad_query, 'wide', axis=0, tiled=True)  6.28 us
    dot_general x4, matrix products, head_scores(): jnp.einsum('ihd,jhd->hij', left_heads, right_heads, preferred_element_typ...  3.87 us
    ppermute x5, waiting for transfers between devices, shifted(): lax.ppermute(value, axis, [(source, source + steps) for source in range(i...  2.34 us
    dot_general x1, matrix products, shards(): jnp.einsum('rtd,rtc->dc', frames, lax.all_gather(grad_query, 'wide', axis...  2.06 us
    dot_general x1, matrix products, shards(): jnp.einsum('hij,ihd->jhd', prior_grad_score, query_heads, preferred_eleme...  1.87 us
  transfers between devices with their start and end apart: 6, of which 2 were waited for; matrix products, arithmetic and copies ran while one was open for 17% of the time, Pallas kernels for 0%

commit v1 on v0

--- a/solution.py
+++ b/solution.py
@@ -85,12 +85,22 @@
     )
     width = frames.shape[2]
     row_block = width // ctx_count
-    panel_sum = jnp.einsum(
-        "rtd,rtc->dc",
-        frames,
-        lax.all_gather(grad_query, "wide", axis=0, tiled=True),
-        preferred_element_type=jnp.float32,
-    )
+    found_now = lax.axis_size("wide")
+    n_now, t1, placed = (found_now, lax.axis_index("wide"), grad_query.shape[0])
+    pile = [(d, (d + 1) % n_now) for d in range(n_now)]
+    spare, panel_sum = (grad_query, None)
+    dd = 0
+    while dd < n_now:
+        formed = lax.ppermute(spare, perm=pile, axis_name="wide") if dd < n_now - 1 else None
+        r1 = jnp.einsum(
+            "rtd,rtc->dc",
+            lax.dynamic_slice_in_dim(frames, (t1 - dd) % n_now * placed, spare.shape[0], axis=0),
+            spare,
+            preferred_element_type=jnp.float32,
+        )
+        panel_sum = r1 if panel_sum is None else panel_sum + r1
+        spare = formed
+        dd += 1
     grad_wq = lax.psum_scatter(panel_sum, "ctx", scatter_dimension=0, tiled=True).reshape(
         1, row_block, columns
     )

time: 79.9 us -> 75.1 us (0.940)
  blocking collectives: 6.28 us -> 0 us
  local copies, waits for them, and re-layouts: 12.1 us -> 8.72 us
  matrix products: 10.5 us -> 13.5 us
  starting transfers between devices: 11.7 us -> 13.7 us
    all_gather x1 -> x0, blocking collectives: 6.28 us -> none  [shards(): lax.all_gather(grad_query, 'wide', axis=0, tiled=True)]
    unnamed x25 -> x18, local copies, waits for them, and re-layouts: 8.25 us -> 4.9 us
    ppermute x5, waiting for transfers between devices: 2.34 us -> 0.01 us  [shifted(): lax.ppermute(value, axis, [(source, source + steps) for source in range(i...]
    ppermute x0 -> x1, waiting for transfers between devices: none -> 2.25 us  [shards(): lax.ppermute(spare, perm=pile, axis_name='wide')]
    ppermute x0 -> x1, starting transfers between devices: none -> 1.5 us  [shards(): lax.ppermute(spare, perm=pile, axis_name='wide')]
    dot_general x1 -> x2, matrix products: 2.06 us -> 3.28 us  [shards(): jnp.einsum('rtd,rtc->dc', lax.dynamic_slice_in_dim(frames, (t1 - dd) % n_...]
    dot_general x1, matrix products: 0.85 us -> 1.75 us  [shards(): jnp.einsum('hij,jhd->ihd', prior_grad_score, prior_key_heads, preferred_e...]
  transfers between devices with their start and end apart: 6 -> 7, of which waited for: 2 -> 2; matrix products, arithmetic and copies ran while one was open for 17% -> 23% of each run, Pallas kernels for 0% -> 0%
where the time goes in v1:
time: 75.1 us; the launch traced here: 74.6 us
  waiting for transfers between devices  23.7 us (32%)
  between operations  14.3 us (19%)
  starting transfers between devices  13.7 us (18%)
  matrix products  13.5 us (18%)
  local copies, waits for them, and re-layouts  8.72 us (12%)
    reduce_scatter x1, waiting for transfers between devices, shards(): lax.psum_scatter(panel_sum, 'ctx', scatter_dimension=0, tiled=True)  21.4 us
    ppermute x5, starting transfers between devices, shifted(): lax.ppermute(value, axis, [(source, source + steps) for source in range(i...  12.2 us
    unnamed x18, local copies, waits for them, and re-layouts  4.9 us
    dot_general x4, matrix products, head_scores(): jnp.einsum('ihd,jhd->hij', left_heads, right_heads, preferred_element_typ...  3.89 us
    dot_general x2, matrix products, shards(): jnp.einsum('rtd,rtc->dc', lax.dynamic_slice_in_dim(frames, (t1 - dd) % n_...  3.28 us
    ppermute x1, waiting for transfers between devices, shards(): lax.ppermute(spare, perm=pile, axis_name='wide')  2.25 us
    dot_general x1, matrix products, shards(): jnp.einsum('hij,ihd->jhd', prior_grad_score, query_heads, preferred_eleme...  1.89 us
    dot_general x1, matrix products, shards(): jnp.einsum('hij,jhd->ihd', prior_grad_score, prior_key_heads, preferred_e...  1.75 us
  transfers between devices with their start and end apart: 7, of which 2 were waited for; matrix products, arithmetic and copies ran while one was open for 23% of the time, Pallas kernels for 0%

profile of v1, /device:TPU:0, one launch (start us, length us, event | category | flops | bytes accessed | tf_op | source)
XLA Modules:
  0.0 74.6 jit_solution(3589378240633850144)
XLA Ops:
  7.2 2.5 %collective-permute-start = (s32[1,256]{1,0:T(1,128)}, s32[1,256]{1,0:T(1,128)S(1)}, u32[]{:S(2)}, u32[]{:S(2)}) collective-permute-start(s32[1,256]{1,0:T(1,128)} %param.10), channel_id=1, source_target_pairs={{0,8},{8,16},{16,24},{1,9},{9,17},{17,25},{2,10},{10,18},{18,26},{... | collective-permute-start | bytes 3080 | tf_op jit(solution)/shard_map/ppermute | solution.py:12
  9.8 1.0 %copy.63 = bf16[1,256,256]{1,2,0:T(8,128)(2,1)S(1)} copy(bf16[1,256,256]{2,1,0:T(8,128)(2,1)} %param.7) | data formatting | bytes 262144 | tf_op jit(solution)/shard_map/reshape | solution.py:27
  10.8 5.2 %collective-permute-start.1 = (bf16[1,256,256]{1,2,0:T(8,128)(2,1)S(1)}, bf16[1,256,256]{1,2,0:T(8,128)(2,1)}, u32[]{:S(2)}, u32[]{:S(2)}) collective-permute-start(bf16[1,256,256]{1,2,0:T(8,128)(2,1)S(1)} %copy.63), channel_id=1, source_target_pairs={{0,8},{8,16},{16,24},{1,9},{9,17},{17,25},{2,10},{10,18},{18,26},{... | collective-permute-start | bytes 393224 | tf_op jit(solution)/shard_map/ppermute | solution.py:12
  16.0 1.7 %copy.38 = bf16[1,256,256]{1,2,0:T(8,128)(2,1)} copy(bf16[1,256,256]{2,1,0:T(8,128)(2,1)} %param.8) | data formatting | bytes 262144 | tf_op args[2]
  17.6 1.9 %collective-permute-start.2 = (bf16[1,256,256]{1,2,0:T(8,128)(2,1)}, bf16[1,256,256]{1,2,0:T(8,128)(2,1)}, u32[]{:S(2)}, u32[]{:S(2)}) collective-permute-start(bf16[1,256,256]{1,2,0:T(8,128)(2,1)} %copy.38), channel_id=1, source_target_pairs={{0,8},{8,16},{16,24},{1,9},{9,17},{17,25},{2,10},{10,18},{18,26},{... | collective-permute-start | bytes 393224 | tf_op jit(solution)/shard_map/ppermute | solution.py:12
  19.6 0.9 %reshape.82 = bf16[256,2,128]{2,1,0:T(2,128)(2,1)S(1)} reshape(bf16[1,256,256]{2,1,0:T(8,128)(2,1)} %param.8) | data formatting | bytes 262144 | tf_op jit(solution)/shard_map/reshape | solution.py:28
  20.5 0.9 %reshape.81 = bf16[256,2,128]{2,1,0:T(2,128)(2,1)S(1)} reshape(bf16[1,256,256]{2,1,0:T(8,128)(2,1)} %param.9) | data formatting | bytes 262144 | tf_op jit(solution)/shard_map/reshape | solution.py:29
  21.5 1.0 %fusion.24 = f32[2,256,256]{1,2,0:T(8,128)} fusion(bf16[256,2,128]{2,1,0:T(2,128)(2,1)S(1)} %reshape.82, bf16[256,2,128]{2,1,0:T(2,128)(2,1)S(1)} %reshape.81), kind=kOutput, calls=%fused_computation.42 | convolution fusion | flops 33554432 | bytes 786432 | tf_op jit(solution)/shard_map/ihd,jhd->hij/dot_general | solution.py:16
  22.5 0.9 %reshape.78 = bf16[256,2,128]{2,1,0:T(2,128)(2,1)S(1)} reshape(bf16[1,256,256]{2,1,0:T(8,128)(2,1)} %param.6) | data formatting | bytes 262144 | tf_op jit(solution)/shard_map/reshape | solution.py:26
  23.9 1.2 %select_reduce_fusion.2 = (f32[2,256]{1,0:T(2,128)S(1)}, f32[2,256,256]{1,2,0:T(8,128)S(1)}) fusion(pred[256,256]{0,1:T(8,128)(4,1)S(1)} %get-tuple-element.18, bf16[256,2,128]{0,2,1:T(8,128)(2,1)} %bitcast.2, bf16[256,2,128]{2,1,0:T(2,128)(2,1)S(1)} %reshape.78), kind=kOutput, calls=%fused_computation.28 | convolution fusion | flops 33947136 | bytes 854016 | tf_op jit(solution)/shard_map/ihd,jhd->hij/dot_general | solution.py:16
  25.4 1.4 %multiply_reduce_fusion = (f32[2,256]{1,0:T(2,128)S(1)}, f32[2,256]{1,0:T(2,128)S(1)}, f32[2,256,256]{1,2,0:T(8,128)S(1)}) fusion(f32[2,256,256]{1,2,0:T(8,128)S(1)} %get-tuple-element.23, f32[2,256]{1,0:T(2,128)S(1)} %log_add_fusion, pred[256,256]{0,1:T(8,128)(4,1)S(1)} %get-tuple-element.18, f32[2,256,256]{1,2,0:T(8,128)S(1)} %copy-done.1, ...), kind=kOutput, calls=%fused_computation.22 | convolution fusion | flops 34601984 | bytes 2496512 | tf_op jit(solution)/shard_map/ihd,jhd->hij/dot_general | solution.py:16
  27.3 1.8 %fusion.6 = bf16[2,256,128]{1,2,0:T(8,128)(2,1)} fusion(f32[2,256,128]{1,2,0:T(8,128)S(1)} %fusion.39, bf16[256,2,128]{0,2,1:T(8,128)(2,1)} %bitcast.2, bf16[2,256,256]{1,2,0:T(8,128)(2,1)S(1)} %get-tuple-element.16), kind=kOutput, calls=%fused_computation.14 | convolution fusion | flops 33751040 | bytes 786432 | tf_op jit(solution)/shard_map/hij,jhd->ihd/dot_general | solution.py:59
  29.1 1.5 %collective-permute-start.5 = (bf16[1,256,256]{1,2,0:T(8,128)(2,1)}, bf16[1,256,256]{1,2,0:T(8,128)(2,1)S(1)}, u32[]{:S(2)}, u32[]{:S(2)}) collective-permute-start(bf16[1,256,256]{1,2,0:T(8,128)(2,1)} %bitcast.5), channel_id=1, source_target_pairs={{0,1},{1,0},{2,3},{3,2},{4,5},{5,4},{6,7},{7,6},{8,9},{9,8},{10,11... | collective-permute-start | bytes 393224 | tf_op jit(solution)/shard_map/ppermute | solution.py:94
  30.6 1.4 %fusion.8 = f32[2048,256]{1,0:T(8,128)S(1)} fusion(bf16[256,256]{0,1:T(8,128)(2,1)} %bitcast.13, bf16[2,256,2048]{2,1,0:T(8,128)(2,1)S(1)} %copy-done, s32[]{:T(128)S(6)} %select_n.43), kind=kOutput, calls=%fused_computation.16 | convolution fusion | flops 268435456 | bytes 3276804 | tf_op jit(solution)/shard_map/rtd,rtc->dc/dot_general | solution.py:95
  32.0 2.3 %collective-permute-done.5 = bf16[1,256,256]{1,2,0:T(8,128)(2,1)S(1)} collective-permute-done((bf16[1,256,256]{1,2,0:T(8,128)(2,1)}, bf16[1,256,256]{1,2,0:T(8,128)(2,1)S(1)}, u32[]{:S(2)}, u32[]{:S(2)}) %collective-permute-start.5) | collective-permute-done | bytes 131104 | tf_op jit(solution)/shard_map/ppermute | solution.py:94
  34.3 1.9 %convolution_add_fusion = f32[2048,256]{1,0:T(8,128)} fusion(f32[2048,256]{1,0:T(8,128)S(1)} %fusion.8, bf16[2,256,2048]{2,1,0:T(8,128)(2,1)S(1)} %copy-done, s32[]{:T(128)S(6)} %select_n.45, bf16[1,256,256]{1,2,0:T(8,128)(2,1)S(1)} %collective-permute-done.5), kind=kOutput, calls=%fused_computation | convolution fusion | flops 268959744 | bytes 5373956 | tf_op jit(solution)/shard_map/rtd,rtc->dc/dot_general | solution.py:95
  36.1 1.9 %convolution_bitcast_fusion.2 = f32[256,2,128]{0,2,1:T(8,128)} fusion(bf16[2,256,256]{1,2,0:T(8,128)(2,1)} %copy-done.3, bf16[256,2,128]{2,1,0:T(2,128)(2,1)S(1)} %reshape.78), kind=kOutput, calls=%fused_computation.8 | convolution fusion | flops 33554432 | bytes 655360 | tf_op jit(solution)/shard_map/hij,ihd->jhd/dot_general | solution.py:70
  38.0 1.3 %collective-permute-start.3 = (f32[256,2,128]{0,2,1:T(8,128)}, f32[256,2,128]{0,2,1:T(8,128)}, u32[]{:S(2)}, u32[]{:S(2)}) collective-permute-start(f32[256,2,128]{0,2,1:T(8,128)} %convolution_bitcast_fusion.2), channel_id=1, source_target_pairs={{8,0},{16,8},{24,16},{9,1},{17,9},{25,17},{10,2},{18,10},{26,18},{... | collective-permute-start | bytes 786440 | tf_op jit(solution)/shard_map/ppermute | solution.py:12
  39.3 1.0 %convolution_bitcast_fusion = f32[256,2,128]{0,2,1:T(8,128)} fusion(f32[2,256,256]{1,2,0:T(8,128)S(1)} %get-tuple-element.23, f32[2,256]{1,0:T(2,128)S(1)} %log_add_fusion, pred[256,256]{0,1:T(8,128)(4,1)S(1)} %get-tuple-element.18, bf16[256,2,128]{2,1,0:T(2,128)(2,1)S(1)} %reshape.81), kind=kOutput, calls=%fused_computation.5 | convolution fusion | flops 33947648 | bytes 985088 | tf_op jit(solution)/shard_map/hij,ihd->jhd/dot_general | solution.py:73
  40.3 1.3 %collective-permute-start.4 = (f32[256,2,128]{0,2,1:T(8,128)}, f32[256,2,128]{0,2,1:T(8,128)S(1)}, u32[]{:S(2)}, u32[]{:S(2)}) collective-permute-start(f32[256,2,128]{0,2,1:T(8,128)} %convolution_bitcast_fusion), channel_id=1, source_target_pairs={{8,0},{16,8},{24,16},{9,1},{17,9},{25,17},{10,2},{18,10},{26,18},{... | collective-permute-start | bytes 786440 | tf_op jit(solution)/shard_map/ppermute | solution.py:12
  41.6 1.7 %copy.52 = bf16[1,256,256]{2,1,0:T(8,128)(2,1)} copy(bf16[1,256,256]{1,2,0:T(8,128)(2,1)} %bitcast.5) | data formatting | bytes 262144
  43.3 1.3 %fusion.4 = bf16[256,2,128]{0,2,1:T(8,128)(2,1)S(1)} fusion(f32[256,2,128]{0,2,1:T(8,128)} %collective-permute-done.3, bf16[2,256,256]{1,2,0:T(8,128)(2,1)} %copy-done.2, bf16[256,2,128]{2,1,0:T(2,128)(2,1)S(1)} %reshape.78), kind=kOutput, calls=%fused_computation.12 | convolution fusion | flops 33751040 | bytes 786432 | tf_op jit(solution)/shard_map/hij,ihd->jhd/dot_general | solution.py:64
  44.6 0.8 %copy.53 = bf16[1,256,256]{2,1,0:T(8,128)(2,1)} copy(bf16[1,256,256]{1,2,0:T(8,128)(2,1)S(1)} %bitcast.53) | data formatting | bytes 262144
  46.4 21.4 %reduce-scatter.2.cloned.1.call-done = f32[512,256]{1,0:T(8,128)} async-done(((f32[2048,256]{1,0:T(8,128)}), f32[512,256]{1,0:T(8,128)}) %reduce-scatter.2.cloned.1.call-update) | async-done | bytes 524304 | tf_op jit(solution)/shard_map/reduce_scatter | solution.py:104
  (31 shorter events, 2.2 us)
Async XLA Ops:
  7.2 23.4 %copy-start = (bf16[2,256,2048]{2,1,0:T(8,128)(2,1)S(1)}, bf16[2,256,2048]{2,1,0:T(8,128)(2,1)}, u32[]{:S(2)}) copy-start(bf16[2,256,2048]{2,1,0:T(8,128)(2,1)} %param.11) | copy-start | bytes 6291460
  7.2 16.3 %copy-start.6 = (s32[1,256]{1,0:T(1,128)S(1)}, s32[1,256]{1,0:T(1,128)}, u32[]{:S(2)}) copy-start(s32[1,256]{1,0:T(1,128)} %param.10) | copy-start | bytes 3076
  7.2 60.6 %reduce-scatter.2.cloned.1.call-start = ((), (), s32[]{:S(2)}) async-start(), calls=%async_computation.1 | async-start | bytes 2621440 | tf_op jit(solution)/shard_map/reduce_scatter | solution.py:104
  7.2 16.2 %collective-permute-start = (s32[1,256]{1,0:T(1,128)}, s32[1,256]{1,0:T(1,128)S(1)}, u32[]{:S(2)}, u32[]{:S(2)}) collective-permute-start(s32[1,256]{1,0:T(1,128)} %param.10), channel_id=1, source_target_pairs={{0,8},{8,16},{16,24},{1,9},{9,17},{17,25},{2,10},{10,18},{18,26},{... | collective-permute-start | bytes 3080 | tf_op jit(solution)/shard_map/ppermute | solution.py:12
  10.8 13.1 %copy-start.4 = (bf16[1,256,256]{1,2,0:T(8,128)(2,1)}, bf16[1,256,256]{1,2,0:T(8,128)(2,1)S(1)}, u32[]{:S(2)}) copy-start(bf16[1,256,256]{1,2,0:T(8,128)(2,1)S(1)} %copy.63) | copy-start | bytes 393220
  10.8 13.1 %collective-permute-start.1 = (bf16[1,256,256]{1,2,0:T(8,128)(2,1)S(1)}, bf16[1,256,256]{1,2,0:T(8,128)(2,1)}, u32[]{:S(2)}, u32[]{:S(2)}) collective-permute-start(bf16[1,256,256]{1,2,0:T(8,128)(2,1)S(1)} %copy.63), channel_id=1, source_target_pairs={{0,8},{8,16},{16,24},{1,9},{9,17},{17,25},{2,10},{10,18},{18,26},{... | collective-permute-start | bytes 393224 | tf_op jit(solution)/shard_map/ppermute | solution.py:12
  17.6 7.8 %collective-permute-start.2 = (bf16[1,256,256]{1,2,0:T(8,128)(2,1)}, bf16[1,256,256]{1,2,0:T(8,128)(2,1)}, u32[]{:S(2)}, u32[]{:S(2)}) collective-permute-start(bf16[1,256,256]{1,2,0:T(8,128)(2,1)} %copy.38), channel_id=1, source_target_pairs={{0,8},{8,16},{16,24},{1,9},{9,17},{17,25},{2,10},{10,18},{18,26},{... | collective-permute-start | bytes 393224 | tf_op jit(solution)/shard_map/ppermute | solution.py:12
  23.4 2.0 %copy-start.1 = (f32[2,256,256]{1,2,0:T(8,128)S(1)}, f32[2,256,256]{1,2,0:T(8,128)}, u32[]{:S(2)}) copy-start(f32[2,256,256]{1,2,0:T(8,128)} %fusion.24) | copy-start | bytes 1572868
  25.4 1.7 %copy-start.5 = (bf16[1,256,256]{1,2,0:T(8,128)(2,1)S(1)}, bf16[1,256,256]{1,2,0:T(8,128)(2,1)}, u32[]{:S(2)}) copy-start(bf16[1,256,256]{1,2,0:T(8,128)(2,1)} %copy-done.4) | copy-start | bytes 393220
  27.1 3.5 %copy-start.2 = (bf16[2,256,256]{1,2,0:T(8,128)(2,1)}, bf16[2,256,256]{1,2,0:T(8,128)(2,1)S(1)}, u32[]{:S(2)}) copy-start(bf16[2,256,256]{1,2,0:T(8,128)(2,1)S(1)} %get-tuple-element.17) | copy-start | bytes 786436
  27.1 3.5 %copy-start.3 = (bf16[2,256,256]{1,2,0:T(8,128)(2,1)}, bf16[2,256,256]{1,2,0:T(8,128)(2,1)S(1)}, u32[]{:S(2)}) copy-start(bf16[2,256,256]{1,2,0:T(8,128)(2,1)S(1)} %get-tuple-element.16) | copy-start | bytes 786436
  29.1 5.2 %collective-permute-start.5 = (bf16[1,256,256]{1,2,0:T(8,128)(2,1)}, bf16[1,256,256]{1,2,0:T(8,128)(2,1)S(1)}, u32[]{:S(2)}, u32[]{:S(2)}) collective-permute-start(bf16[1,256,256]{1,2,0:T(8,128)(2,1)} %bitcast.5), channel_id=1, source_target_pairs={{0,1},{1,0},{2,3},{3,2},{4,5},{5,4},{6,7},{7,6},{8,9},{9,8},{10,11... | collective-permute-start | bytes 393224 | tf_op jit(solution)/shard_map/ppermute | solution.py:94
  38.0 5.2 %collective-permute-start.3 = (f32[256,2,128]{0,2,1:T(8,128)}, f32[256,2,128]{0,2,1:T(8,128)}, u32[]{:S(2)}, u32[]{:S(2)}) collective-permute-start(f32[256,2,128]{0,2,1:T(8,128)} %convolution_bitcast_fusion.2), channel_id=1, source_target_pairs={{8,0},{16,8},{24,16},{9,1},{17,9},{25,17},{10,2},{18,10},{26,18},{... | collective-permute-start | bytes 786440 | tf_op jit(solution)/shard_map/ppermute | solution.py:12
  40.3 5.1 %collective-permute-start.4 = (f32[256,2,128]{0,2,1:T(8,128)}, f32[256,2,128]{0,2,1:T(8,128)S(1)}, u32[]{:S(2)}, u32[]{:S(2)}) collective-permute-start(f32[256,2,128]{0,2,1:T(8,128)} %convolution_bitcast_fusion), channel_id=1, source_target_pairs={{8,0},{16,8},{24,16},{9,1},{17,9},{25,17},{10,2},{18,10},{26,18},{... | collective-permute-start | bytes 786440 | tf_op jit(solution)/shard_map/ppermute | solution.py:12
Sparse Core Ops, SparseCore 0:
  36.3 31.4 reduce-scatter.1
